TPU v7x, 32 devices: a whole 2x2x4 slice. The times are simulated.
32 devices in a mesh: groups: 2 (over y), seq: 4 (over z), rep: 2 (over x), fsdp: 2 (over core).
Axes of the slice: x: 2, y: 2, z: 4, core: 2. Of those that a mesh axis runs over, the one named last changes fastest.
Arguments:
- activations: bfloat16 [8, 512, 2048], P(('groups', 'rep', 'fsdp'), 'seq'), parts along dimension 0, may hold values from -6 to 6
- queries: bfloat16 [8, 512, 2048], P(('groups', 'rep', 'fsdp'), 'seq'), parts along dimension 0, may hold values from -102 to 102
- key_weight: bfloat16 [2048, 512], P(('seq', 'fsdp')), may hold values from -0.125 to 0.125
- value_weight: bfloat16 [2048, 512], P(('seq', 'fsdp')), may hold values from -0.125 to 0.125
- segment_ids: int32 [8, 512], P(('groups', 'rep', 'fsdp'), 'seq'), parts along dimension 0, may hold values from 0 to 3, never falling along the last dimension, each value on 1 to 384 neighbouring positions
- out_grad: bfloat16 [8, 512, 2048], P(('groups', 'rep', 'fsdp'), 'seq'), parts along dimension 0, may hold values from -6 to 6
Outputs:
- context: bfloat16 [8, 512, 2048], P(('groups', 'rep', 'fsdp'), 'seq'), parts along dimension 0
- query_grad: bfloat16 [8, 512, 2048], P(('groups', 'rep', 'fsdp'), 'seq'), parts along dimension 0
- input_grad: bfloat16 [8, 512, 2048], P(('groups', 'rep', 'fsdp'), 'seq'), parts along dimension 0
- key_weight_grad: bfloat16 [4096, 512], P(('groups', 'seq', 'fsdp')), parts along dimension 0
- value_weight_grad: bfloat16 [4096, 512], P(('groups', 'seq', 'fsdp')), parts along dimension 0
There are 2 independent parts, one for each index of `groups`. A program takes and returns all parts, laid end to end along the dimension named above; an argument that names none is the same for every part. Nothing has to cross between parts.
Inputs may be any that keep to these rules, and one draw needn't show every extreme that they name: `segment_ids`: document numbers never fall along a sequence; a document covers at most 384 positions.
All inputs are finite; a program needn't handle non-finite values.
Results may differ from a plain program's by a relative error of at most 0.025.
The roundings to bfloat16 on the way count: a program that leaves them out, or rounds other values in their place, can miss the bound.
Values may be sent and summed in bfloat16 or wider, within the bound.
No kernel may reach another device: no remote copies, remote signals or barrier semaphores. Data moves between devices by JAX's collectives and lax.ppermute only.
A program may use at most 64 MiB of HBM per device.

v0:
```python
import math
import jax
import jax.numpy as jnp
from jax import lax
from jax.sharding import PartitionSpec as P

HEADS = 16
KV_HEADS = 4
HEAD_DIM = 128
masked_low = -1e30


def block_mask(seg_all, row_start, col_start, block_width):
    row_pos = row_start + lax.iota(jnp.int32, block_width)
    col_pos = col_start + lax.iota(jnp.int32, block_width)
    seg_rows = lax.dynamic_slice_in_dim(seg_all, row_start, block_width)
    seg_cols = lax.dynamic_slice_in_dim(seg_all, col_start, block_width)
    return (col_pos[None, :] <= row_pos[:, None]) & (seg_cols[None, :] == seg_rows[:, None])


def block_scores(query_block, key_block, inv_root):
    return (
        jnp.einsum("qhd,khd->hqk", query_block, key_block, preferred_element_type=jnp.float32)
        * inv_root
    )


def take_block(source, index, block_width):
    return lax.dynamic_slice_in_dim(source, index * block_width, block_width, 0)


def attend(query_part, key_part, value_part, seg_all):
    length, heads_here, head_size = query_part.shape
    block_width = min(512, length)
    block_count = length // block_width
    inv_root = 1.0 / math.sqrt(head_size)

    def stats_row(i, log_totals):
        query_block = take_block(query_part, i, block_width)

        def stats_inner(j, state_now):
            running_max, running_sum = state_now
            scores = block_scores(query_block, take_block(key_part, j, block_width), inv_root)
            allowed = block_mask(seg_all, i * block_width, j * block_width, block_width)[None]
            scores = jnp.where(allowed, scores, masked_low)
            new_max = jnp.maximum(running_max, jnp.max(scores, axis=-1))
            weights = jnp.where(allowed, jnp.exp(scores - new_max[..., None]), 0.0)
            running_sum = running_sum * jnp.exp(running_max - new_max) + jnp.sum(weights, axis=-1)
            return (new_max, running_sum)

        start_state = (
            jnp.full((heads_here, block_width), masked_low, jnp.float32),
            jnp.zeros((heads_here, block_width), jnp.float32),
        )
        running_max, running_sum = lax.fori_loop(0, i + 1, stats_inner, start_state)
        return lax.dynamic_update_slice_in_dim(
            log_totals, running_max + jnp.log(running_sum), i * block_width, 1
        )

    log_totals = lax.fori_loop(
        0, block_count, stats_row, jnp.zeros((heads_here, length), jnp.float32)
    )

    def out_row(i, out_all):
        query_block = take_block(query_part, i, block_width)
        log_block = lax.dynamic_slice_in_dim(log_totals, i * block_width, block_width, 1)

        def out_inner(j, accum_out):
            scores = block_scores(query_block, take_block(key_part, j, block_width), inv_root)
            allowed = block_mask(seg_all, i * block_width, j * block_width, block_width)[None]
            probs_low = jnp.where(allowed, jnp.exp(scores - log_block[..., None]), 0.0).astype(
                jnp.bfloat16
            )
            return accum_out + jnp.einsum(
                "hqk,khd->qhd",
                probs_low,
                take_block(value_part, j, block_width),
                preferred_element_type=jnp.float32,
            )

        accum_out = lax.fori_loop(
            0, i + 1, out_inner, jnp.zeros((block_width, heads_here, head_size), jnp.float32)
        )
        return lax.dynamic_update_slice_in_dim(
            out_all, accum_out.astype(jnp.bfloat16), i * block_width, 0
        )

    out_all = lax.fori_loop(
        0, block_count, out_row, jnp.zeros((length, heads_here, head_size), jnp.bfloat16)
    )
    return (out_all, log_totals)


def attend_grads(query_part, key_part, value_part, seg_all, out_part, log_totals, grad_part):
    length, heads_here, head_size = query_part.shape
    block_width = min(512, length)
    block_count = length // block_width
    inv_root = 1.0 / math.sqrt(head_size)
    row_dots = jnp.einsum("qhd,qhd->hq", grad_part, out_part, preferred_element_type=jnp.float32)

    def grad_row(i, state_now):
        query_all, key_all, value_all = state_now
        query_block = take_block(query_part, i, block_width)
        grad_block = take_block(grad_part, i, block_width)
        log_block = lax.dynamic_slice_in_dim(log_totals, i * block_width, block_width, 1)
        dots_block = lax.dynamic_slice_in_dim(row_dots, i * block_width, block_width, 1)

        def grad_inner(j, inner_state):
            query_accum, key_accum, value_accum = inner_state
            key_block = take_block(key_part, j, block_width)
            value_block = take_block(value_part, j, block_width)
            scores = block_scores(query_block, key_block, inv_root)
            allowed = block_mask(seg_all, i * block_width, j * block_width, block_width)[None]
            probs = jnp.where(allowed, jnp.exp(scores - log_block[..., None]), 0.0)
            probs_low = probs.astype(jnp.bfloat16)
            value_new = take_block(value_accum, j, block_width) + jnp.einsum(
                "hqk,qhd->khd", probs_low, grad_block, preferred_element_type=jnp.float32
            )
            value_accum = lax.dynamic_update_slice_in_dim(
                value_accum, value_new, j * block_width, 0
            )
            prob_grad = jnp.einsum(
                "qhd,khd->hqk", grad_block, value_block, preferred_element_type=jnp.float32
            )
            score_grad = (probs * (prob_grad - dots_block[..., None])).astype(jnp.bfloat16)
            query_accum = query_accum + jnp.einsum(
                "hqk,khd->qhd", score_grad, key_block, preferred_element_type=jnp.float32
            )
            key_new = take_block(key_accum, j, block_width) + jnp.einsum(
                "hqk,qhd->khd", score_grad, query_block, preferred_element_type=jnp.float32
            )
            key_accum = lax.dynamic_update_slice_in_dim(key_accum, key_new, j * block_width, 0)
            return (query_accum, key_accum, value_accum)

        start_state = (
            jnp.zeros((block_width, heads_here, head_size), jnp.float32),
            key_all,
            value_all,
        )
        query_accum, key_all, value_all = lax.fori_loop(0, i + 1, grad_inner, start_state)
        query_all = lax.dynamic_update_slice_in_dim(
            query_all, (query_accum * inv_root).astype(jnp.bfloat16), i * block_width, 0
        )
        return (query_all, key_all, value_all)

    zero_grads = jnp.zeros((length, heads_here, head_size), jnp.float32)
    start_all = (jnp.zeros((length, heads_here, head_size), jnp.bfloat16), zero_grads, zero_grads)
    query_all, key_all, value_all = lax.fori_loop(0, block_count, grad_row, start_all)
    return (query_all, (key_all * inv_root).astype(jnp.bfloat16), value_all.astype(jnp.bfloat16))


def body(activations, queries, key_weight, value_weight, segment_ids, out_grad):
    rows_here = activations.shape[1]
    inputs = activations[0]
    kv_width = key_weight.shape[1]
    seq_devices = lax.axis_size("seq")
    heads_here = HEADS // seq_devices
    kv_group = HEADS // KV_HEADS
    stacked = jnp.concatenate([key_weight, value_weight], axis=1)
    columns = inputs
    projected = jnp.dot(
        columns,
        lax.all_gather(stacked, ("seq", "fsdp"), axis=0, tiled=True),
        preferred_element_type=jnp.float32,
    )
    projected = projected.astype(jnp.bfloat16)
    key_rows = projected[:, :kv_width].reshape(rows_here, KV_HEADS, HEAD_DIM)
    value_rows = projected[:, kv_width:].reshape(rows_here, KV_HEADS, HEAD_DIM)
    kv_copies = max(kv_group // heads_here, 1)
    query_heads = queries[0].reshape(rows_here, HEADS, HEAD_DIM)
    sent = (
        query_heads,
        jnp.repeat(key_rows, kv_copies, axis=1),
        jnp.repeat(value_rows, kv_copies, axis=1),
    )
    query_part, key_part, value_part = (
        lax.all_to_all(sent[0], "seq", split_axis=1, concat_axis=0, tiled=True),
        lax.all_to_all(sent[1], "seq", split_axis=1, concat_axis=0, tiled=True),
        lax.all_to_all(sent[2], "seq", split_axis=1, concat_axis=0, tiled=True),
    )
    widen_by = heads_here // key_part.shape[1]
    key_part = jnp.repeat(key_part, widen_by, axis=1)
    value_part = jnp.repeat(value_part, widen_by, axis=1)
    seg_all = lax.all_gather(segment_ids[0], "seq", axis=0, tiled=True)
    out_part, log_totals = attend(query_part, key_part, value_part, seg_all)
    context = lax.all_to_all(out_part, "seq", split_axis=0, concat_axis=1, tiled=True).reshape(
        1, rows_here, HEADS * HEAD_DIM
    )
    grad_part = lax.all_to_all(
        out_grad[0].reshape(rows_here, HEADS, HEAD_DIM),
        "seq",
        split_axis=1,
        concat_axis=0,
        tiled=True,
    )
    query_back, key_back, value_back = attend_grads(
        query_part, key_part, value_part, seg_all, out_part, log_totals, grad_part
    )
    query_tok, key_tok, value_tok = (
        lax.all_to_all(query_back, "seq", split_axis=0, concat_axis=1, tiled=True),
        lax.all_to_all(key_back, "seq", split_axis=0, concat_axis=1, tiled=True),
        lax.all_to_all(value_back, "seq", split_axis=0, concat_axis=1, tiled=True),
    )
    key_sum = (
        key_tok.reshape(rows_here, KV_HEADS, kv_group, HEAD_DIM).astype(jnp.float32).sum(axis=2)
    )
    value_sum = (
        value_tok.reshape(rows_here, KV_HEADS, kv_group, HEAD_DIM).astype(jnp.float32).sum(axis=2)
    )
    grad_kv = jnp.concatenate(
        [
            key_sum.astype(jnp.bfloat16).reshape(rows_here, kv_width),
            value_sum.astype(jnp.bfloat16).reshape(rows_here, kv_width),
        ],
        axis=1,
    )
    input_grad = lax.dot_general(
        grad_kv,
        lax.all_gather(stacked, ("seq", "fsdp"), axis=0, tiled=True),
        (((1,), (1,)), ((), ())),
        preferred_element_type=jnp.float32,
    )
    input_grad = input_grad.astype(jnp.bfloat16).reshape(1, rows_here, inputs.shape[1])
    columns = inputs
    grad_shard = lax.psum_scatter(
        lax.dot_general(
            columns, grad_kv, (((0,), (0,)), ((), ())), preferred_element_type=jnp.float32
        ).astype(jnp.bfloat16),
        ("seq", "fsdp"),
        scatter_dimension=0,
        tiled=True,
    ).astype(jnp.float32)
    grad_total = lax.psum(grad_shard, "rep").astype(jnp.bfloat16)
    query_grad = query_tok.reshape(1, rows_here, HEADS * HEAD_DIM)
    return (context, query_grad, input_grad, grad_total[:, :kv_width], grad_total[:, kv_width:])


def solution(mesh):
    return jax.shard_map(
        body,
        mesh=mesh,
        in_specs=(
            P(("groups", "rep", "fsdp"), "seq", None),
            P(("groups", "rep", "fsdp"), "seq", None),
            P(("seq", "fsdp"), None),
            P(("seq", "fsdp"), None),
            P(("groups", "rep", "fsdp"), "seq"),
            P(("groups", "rep", "fsdp"), "seq", None),
        ),
        out_specs=(
            P(("groups", "rep", "fsdp"), "seq", None),
            P(("groups", "rep", "fsdp"), "seq", None),
            P(("groups", "rep", "fsdp"), "seq", None),
            P(("groups", "seq", "fsdp"), None),
            P(("groups", "seq", "fsdp"), None),
        ),
        check_vma=False,
    )
```

profile of v0, /device:TPU:0, one launch (start us, length us, event | category | flops | bytes accessed | tf_op | source)
XLA Modules:
  0.0 248.5 jit_solution(1533762481953320926)
XLA Ops:
  7.2 0.0 copy-start
  7.2 0.0 all-gather.3.cloned.1.call-start
  7.2 1.9 pad_maximum_fusion
  9.2 0.0 all-gather.3.cloned.1.call-update
  9.2 2.0 copy.45
  11.2 6.3 %all-to-all-start.1 = ((bf16[128,16,128]{0,2,1:T(8,128)(2,1)}), bf16[128,16,128]{0,2,1:T(8,128)(2,1)S(1)}, u32[]{:S(2)}, u32[]{:S(2)}) async-start(bf16[128,16,128]{0,2,1:T(8,128)(2,1)} %bitcast.9), calls=%async_computation.1 | async-start | bytes 1048576 | tf_op jit(solution)/shard_map/all_to_all | solution.py:177
  17.5 2.0 copy.52
  19.6 24.7 %all-to-all-done.1 = bf16[128,16,128]{0,2,1:T(8,128)(2,1)S(1)} async-done(((bf16[128,16,128]{0,2,1:T(8,128)(2,1)}), bf16[128,16,128]{0,2,1:T(8,128)(2,1)S(1)}, u32[]{:S(2)}, u32[]{:S(2)}) %all-to-all-start.1) | async-done | bytes 524320 | tf_op jit(solution)/shard_map/all_to_all | solution.py:177
  44.2 3.6 %all-to-all-start.4 = ((bf16[128,16,128]{0,2,1:T(8,128)(2,1)}), bf16[128,16,128]{0,2,1:T(8,128)(2,1)S(1)}, u32[]{:S(2)}, u32[]{:S(2)}) async-start(bf16[128,16,128]{0,2,1:T(8,128)(2,1)} %bitcast.22), calls=%async_computation.4 | async-start | bytes 1048576 | tf_op jit(solution)/shard_map/all_to_all | solution.py:189
  47.9 0.0 copy-done.3
  47.9 21.7 %all-gather = s32[1,512]{1,0:T(1,128)S(1)} all-gather(s32[1,128]{1,0:T(1,128)S(1)} %copy-done.3), channel_id=2, replica_groups=mesh['groups'=2,'seq'=4,'rep'=2,'fsdp'=2] {'seq'}, dimensions={1}, use_global_device_ids=true | all-gather | bytes 2560 | tf_op jit(solution)/shard_map/all_gather | solution.py:184
  69.5 9.1 %all-gather.3.cloned.1.call-done = bf16[2048,1024]{1,0:T(8,128)(2,1)} async-done(((bf16[256,1024]{1,0:T(8,128)(2,1)}), bf16[2048,1024]{1,0:T(8,128)(2,1)}) %all-gather.3.cloned.1.call-update) | async-done | bytes 4194320 | tf_op jit(solution)/shard_map/all_gather | solution.py:163
  78.7 0.0 copy-done
  78.7 3.5 %fusion.11 = bf16[128,1024]{0,1:T(8,128)(2,1)S(1)} fusion(bf16[2048,1024]{1,0:T(8,128)(2,1)} %all-gather.3.cloned.1.call-done, bf16[1,128,2048]{2,1,0:T(8,128)(2,1)S(1)} %copy-done), kind=kOutput, calls=%fused_computation.22 | convolution fusion | flops 537001984 | bytes 4980736 | tf_op jit(solution)/shard_map/dot_general | solution.py:161
  82.2 0.8 copy.44
  83.0 0.0 all-to-all-done.4
  83.0 3.3 %all-to-all-start = ((bf16[128,4,128]{2,0,1:T(8,128)(2,1)}), bf16[128,4,128]{2,0,1:T(8,128)(2,1)S(1)}, u32[]{:S(2)}, u32[]{:S(2)}) async-start(bf16[128,4,128]{2,0,1:T(8,128)(2,1)} %copy.44), calls=%async_computation | async-start | bytes 262144 | tf_op jit(solution)/shard_map/all_to_all | solution.py:178
  86.3 0.2 fusion.13
  86.5 0.3 copy.47
  86.8 0.3 copy.54
  87.1 0.8 copy.48
  87.9 4.8 %all-to-all-done = bf16[128,4,128]{2,0,1:T(8,128)(2,1)S(1)} async-done(((bf16[128,4,128]{2,0,1:T(8,128)(2,1)}), bf16[128,4,128]{2,0,1:T(8,128)(2,1)S(1)}, u32[]{:S(2)}, u32[]{:S(2)}) %all-to-all-start) | async-done | bytes 131104 | tf_op jit(solution)/shard_map/all_to_all | solution.py:178
  92.7 3.3 %all-to-all-start.2 = ((bf16[128,4,128]{2,0,1:T(8,128)(2,1)}), bf16[128,4,128]{2,0,1:T(8,128)(2,1)S(1)}, u32[]{:S(2)}, u32[]{:S(2)}) async-start(bf16[128,4,128]{2,0,1:T(8,128)(2,1)} %copy.48), calls=%async_computation.2 | async-start | bytes 262144 | tf_op jit(solution)/shard_map/all_to_all | solution.py:179
  96.0 0.9 fusion.3
  96.9 0.0 copy-start.1
  96.9 1.0 select_reduce_fusion
  98.0 0.9 fusion.10
  99.0 0.0 copy-done.1
  99.0 1.2 copy.60
  100.2 1.8 all-to-all-done.2
  101.9 3.5 %all-to-all-start.7 = ((bf16[512,4,128]{2,1,0:T(4,128)(2,1)}), bf16[512,4,128]{2,1,0:T(4,128)(2,1)S(1)}, u32[]{:S(2)}, u32[]{:S(2)}) async-start(bf16[512,4,128]{2,1,0:T(4,128)(2,1)} %copy.60), calls=%async_computation.7 | async-start | bytes 1048576 | tf_op jit(solution)/shard_map/all_to_all | solution.py:202
  105.4 3.9 %fusion.12 = (f32[4,512]{1,0:T(4,128)S(1)}, bf16[4,512,128]{2,1,0:T(8,128)(2,1)S(1)}) fusion(bf16[4,128,4,128]{3,1,0,2:T(8,128)(2,1)S(1)} %copy.54, bf16[512,128]{1,0:T(8,128)(2,1)S(1)} %bitcast.111, f32[4,512,512]{2,1,0:T(8,128)} %copy-done.1, f32[4,512]{1,0:T(4,128)S(1)} %log_add_fusion, pred[512,512]{0,1:T(8,128)(4,1)S(1)} %fusion.13), kind=kOutput, calls=%fused_computation.24 | convolution fusion | flops 273938432 | bytes 5652480 | tf_op jit(solution)/shard_map/while/body/eval_jaxpr/while/body/hqk,khd->qhd/dot_general | solution.py:74
  109.3 1.4 fusion
  110.8 0.7 fusion.8
  111.5 0.6 copy-done.4
  112.1 1.2 copy.58
  113.3 5.2 %all-to-all-done.7 = bf16[512,4,128]{2,1,0:T(4,128)(2,1)S(1)} async-done(((bf16[512,4,128]{2,1,0:T(4,128)(2,1)}), bf16[512,4,128]{2,1,0:T(4,128)(2,1)S(1)}, u32[]{:S(2)}, u32[]{:S(2)}) %all-to-all-start.7) | async-done | bytes 524320 | tf_op jit(solution)/shard_map/all_to_all | solution.py:202
  118.5 3.5 %all-to-all-start.6 = ((bf16[512,4,128]{2,1,0:T(4,128)(2,1)}), bf16[512,4,128]{2,1,0:T(4,128)(2,1)S(1)}, u32[]{:S(2)}, u32[]{:S(2)}) async-start(bf16[512,4,128]{2,1,0:T(4,128)(2,1)} %copy.58), calls=%async_computation.6 | async-start | bytes 1048576 | tf_op jit(solution)/shard_map/all_to_all | solution.py:201
  122.0 0.2 reduce-scatter.2.cloned.1.call-start
  122.2 0.7 reduce_sum.48
  122.9 0.1 copy.61
  123.0 12.3 %all-to-all-done.6 = bf16[512,4,128]{2,1,0:T(4,128)(2,1)S(1)} async-done(((bf16[512,4,128]{2,1,0:T(4,128)(2,1)}), bf16[512,4,128]{2,1,0:T(4,128)(2,1)S(1)}, u32[]{:S(2)}, u32[]{:S(2)}) %all-to-all-start.6) | async-done | bytes 524320 | tf_op jit(solution)/shard_map/all_to_all | solution.py:201
  135.3 0.7 reduce_sum.45
  136.0 0.1 copy.59
  136.1 3.2 %convert_bitcast_fusion = bf16[2048,1024]{0,1:T(8,128)(2,1)} fusion(bf16[1,128,2048]{2,1,0:T(8,128)(2,1)S(1)} %copy-done, bf16[128,512]{0,1:T(8,128)(2,1)S(1)} %bitcast.98, bf16[128,512]{0,1:T(8,128)(2,1)S(1)} %bitcast.100), kind=kOutput, calls=%fused_computation.6 | convolution fusion | flops 539492352 | bytes 4980736 | tf_op jit(solution)/shard_map/dot_general | solution.py:226
  139.3 0.0 reduce-scatter.2.cloned.1.call-update
  139.4 1.2 copy.50
  140.6 3.5 %all-to-all-start.3 = ((bf16[512,4,128]{2,1,0:T(4,128)(2,1)}), bf16[512,4,128]{2,1,0:T(4,128)(2,1)S(1)}, u32[]{:S(2)}, u32[]{:S(2)}) async-start(bf16[512,4,128]{2,1,0:T(4,128)(2,1)} %copy.50), calls=%async_computation.3 | async-start | bytes 1048576 | tf_op jit(solution)/shard_map/all_to_all | solution.py:186
  144.1 0.9 fusion.9
  145.0 1.2 copy.56
  146.2 19.1 %all-to-all-done.3 = bf16[512,4,128]{2,1,0:T(4,128)(2,1)S(1)} async-done(((bf16[512,4,128]{2,1,0:T(4,128)(2,1)}), bf16[512,4,128]{2,1,0:T(4,128)(2,1)S(1)}, u32[]{:S(2)}, u32[]{:S(2)}) %all-to-all-start.3) | async-done | bytes 524320 | tf_op jit(solution)/shard_map/all_to_all | solution.py:186
  165.3 4.3 %all-to-all-start.5 = ((bf16[512,4,128]{2,1,0:T(4,128)(2,1)}), bf16[512,4,128]{2,1,0:T(4,128)(2,1)S(1)}, u32[]{:S(2)}, u32[]{:S(2)}) async-start(bf16[512,4,128]{2,1,0:T(4,128)(2,1)} %copy.56), calls=%async_computation.5 | async-start | bytes 1048576 | tf_op jit(solution)/shard_map/all_to_all | solution.py:200
  169.6 34.6 %reduce-scatter.2.cloned.1.call-done = bf16[256,1024]{0,1:T(8,128)(2,1)} async-done(((bf16[2048,1024]{0,1:T(8,128)(2,1)}), bf16[256,1024]{0,1:T(8,128)(2,1)}) %reduce-scatter.2.cloned.1.call-update) | async-done | bytes 524304 | tf_op jit(solution)/shard_map/reduce_scatter | solution.py:225
  204.2 0.0 all-reduce.2.cloned.1.call-update
  204.2 0.2 copy.51
  204.4 1.2 reshape.232
  205.6 0.0 all-to-all-done.5
  205.6 0.2 copy.57
  205.8 1.2 reshape.233
  207.0 4.5 %fusion.5 = bf16[1,128,2048]{2,1,0:T(8,128)(2,1)} fusion(bf16[2048,1024]{1,0:T(8,128)(2,1)} %all-gather.3.cloned.1.call-done, bf16[128,512]{0,1:T(8,128)(2,1)S(1)} %bitcast.99, bf16[128,512]{0,1:T(8,128)(2,1)S(1)} %bitcast.101), kind=kOutput, calls=%fused_computation.11 | convolution fusion | flops 537657344 | bytes 4980736 | tf_op jit(solution)/shard_map/dot_general | solution.py:217
  211.5 27.7 %all-reduce.2.cloned.1.call-done = bf16[256,1024]{0,1:T(8,128)(2,1)} async-done(((bf16[256,1024]{0,1:T(8,128)(2,1)}), bf16[256,1024]{0,1:T(8,128)(2,1)}) %all-reduce.2.cloned.1.call-update) | async-done | bytes 524304 | tf_op jit(solution)/shard_map/psum | solution.py:233
  239.2 1.1 fusion.25
  240.2 0.8 copy.63
  241.1 0.8 copy.62
  (10 shorter events, 0.1 us)
Async XLA Ops:
  7.2 71.5 %copy-start = (bf16[1,128,2048]{2,1,0:T(8,128)(2,1)S(1)}, bf16[1,128,2048]{2,1,0:T(8,128)(2,1)}, u32[]{:S(2)}) copy-start(bf16[1,128,2048]{2,1,0:T(8,128)(2,1)} %param.6) | copy-start | bytes 1572868
  7.2 40.7 %copy-start.3 = (s32[1,128]{1,0:T(1,128)S(1)}, s32[1,128]{1,0:T(1,128)}, u32[]{:S(2)}) copy-start(s32[1,128]{1,0:T(1,128)} %param.10) | copy-start | bytes 1540
  7.2 71.5 %all-gather.3.cloned.1.call-start = ((), (), s32[]{:S(2)}) async-start(), calls=%async_computation.9 | async-start | bytes 4718592 | tf_op jit(solution)/shard_map/all_gather | solution.py:163
  11.2 33.0 %all-to-all-start.1 = ((bf16[128,16,128]{0,2,1:T(8,128)(2,1)}), bf16[128,16,128]{0,2,1:T(8,128)(2,1)S(1)}, u32[]{:S(2)}, u32[]{:S(2)}) async-start(bf16[128,16,128]{0,2,1:T(8,128)(2,1)} %bitcast.9), calls=%async_computation.1 | async-start | bytes 1048576 | tf_op jit(solution)/shard_map/all_to_all | solution.py:177
  44.2 38.7 %all-to-all-start.4 = ((bf16[128,16,128]{0,2,1:T(8,128)(2,1)}), bf16[128,16,128]{0,2,1:T(8,128)(2,1)S(1)}, u32[]{:S(2)}, u32[]{:S(2)}) async-start(bf16[128,16,128]{0,2,1:T(8,128)(2,1)} %bitcast.22), calls=%async_computation.4 | async-start | bytes 1048576 | tf_op jit(solution)/shard_map/all_to_all | solution.py:189
  83.0 9.7 %all-to-all-start = ((bf16[128,4,128]{2,0,1:T(8,128)(2,1)}), bf16[128,4,128]{2,0,1:T(8,128)(2,1)S(1)}, u32[]{:S(2)}, u32[]{:S(2)}) async-start(bf16[128,4,128]{2,0,1:T(8,128)(2,1)} %copy.44), calls=%async_computation | async-start | bytes 262144 | tf_op jit(solution)/shard_map/all_to_all | solution.py:178
  92.7 9.2 %all-to-all-start.2 = ((bf16[128,4,128]{2,0,1:T(8,128)(2,1)}), bf16[128,4,128]{2,0,1:T(8,128)(2,1)S(1)}, u32[]{:S(2)}, u32[]{:S(2)}) async-start(bf16[128,4,128]{2,0,1:T(8,128)(2,1)} %copy.48), calls=%async_computation.2 | async-start | bytes 262144 | tf_op jit(solution)/shard_map/all_to_all | solution.py:179
  96.9 2.0 copy-start.1
  101.9 16.6 %all-to-all-start.7 = ((bf16[512,4,128]{2,1,0:T(4,128)(2,1)}), bf16[512,4,128]{2,1,0:T(4,128)(2,1)S(1)}, u32[]{:S(2)}, u32[]{:S(2)}) async-start(bf16[512,4,128]{2,1,0:T(4,128)(2,1)} %copy.60), calls=%async_computation.7 | async-start | bytes 1048576 | tf_op jit(solution)/shard_map/all_to_all | solution.py:202
  105.4 3.9 %copy-start.2 = (f32[4,512,512]{2,1,0:T(8,128)S(1)}, f32[4,512,512]{2,1,0:T(8,128)}, u32[]{:S(2)}) copy-start(f32[4,512,512]{2,1,0:T(8,128)} %copy-done.1) | copy-start | bytes 12582916
  110.7 1.4 copy-start.4
  118.5 16.8 %all-to-all-start.6 = ((bf16[512,4,128]{2,1,0:T(4,128)(2,1)}), bf16[512,4,128]{2,1,0:T(4,128)(2,1)S(1)}, u32[]{:S(2)}, u32[]{:S(2)}) async-start(bf16[512,4,128]{2,1,0:T(4,128)(2,1)} %copy.58), calls=%async_computation.6 | async-start | bytes 1048576 | tf_op jit(solution)/shard_map/all_to_all | solution.py:201
  122.0 82.2 %reduce-scatter.2.cloned.1.call-start = ((), (), s32[]{:S(2)}) async-start(), calls=%async_computation.10 | async-start | bytes 4718592 | tf_op jit(solution)/shard_map/reduce_scatter | solution.py:225
  139.3 4.7 %copy-start.5 = (bf16[4,512,512]{1,2,0:T(8,128)(2,1)S(1)}, bf16[4,512,512]{1,2,0:T(8,128)(2,1)}, u32[]{:S(2)}) copy-start(bf16[4,512,512]{1,2,0:T(8,128)(2,1)} %copy-done.4) | copy-start | bytes 6291460
  140.6 24.7 %all-to-all-start.3 = ((bf16[512,4,128]{2,1,0:T(4,128)(2,1)}), bf16[512,4,128]{2,1,0:T(4,128)(2,1)S(1)}, u32[]{:S(2)}, u32[]{:S(2)}) async-start(bf16[512,4,128]{2,1,0:T(4,128)(2,1)} %copy.50), calls=%async_computation.3 | async-start | bytes 1048576 | tf_op jit(solution)/shard_map/all_to_all | solution.py:186
  165.3 40.3 %all-to-all-start.5 = ((bf16[512,4,128]{2,1,0:T(4,128)(2,1)}), bf16[512,4,128]{2,1,0:T(4,128)(2,1)S(1)}, u32[]{:S(2)}, u32[]{:S(2)}) async-start(bf16[512,4,128]{2,1,0:T(4,128)(2,1)} %copy.56), calls=%async_computation.5 | async-start | bytes 1048576 | tf_op jit(solution)/shard_map/all_to_all | solution.py:200
  169.6 69.6 %all-reduce.2.cloned.1.call-start = ((), (), s32[]{:S(2)}) async-start(), calls=%async_computation.11 | async-start | bytes 1048576 | tf_op jit(solution)/shard_map/psum | solution.py:233
Sparse Core Ops, SparseCore 0:
  10.2 68.4 all-gather.2
  139.5 64.6 reduce-scatter.1
  206.5 32.6 all-reduce.1
where the time goes:
time: 249 us; the launch traced here: 248 us
  waiting for transfers between devices  139 us (56%)
  starting transfers between devices  31.6 us (13%)
  blocking collectives  21.7 us (9%)
  matrix products  19.9 us (8%)
  local copies, waits for them, and re-layouts  17.4 us (7%)
  between operations  14 us (6%)
  other arithmetic  4.52 us (2%)
    reduce_scatter x1, waiting for transfers between devices, body(): lax.psum_scatter(lax.dot_general(columns, grad_kv, (((0,), (0,)), ((), ()...  34.6 us
    psum x1, waiting for transfers between devices, body(): grad_total = lax.psum(grad_shard, 'rep').astype(jnp.bfloat16)  27.7 us
    all_to_all x1, waiting for transfers between devices, body(): lax.all_to_all(sent[0], 'seq', split_axis=1, concat_axis=0, tiled=True)  24.7 us
    all_gather x1, blocking collectives, body(): seg_all = lax.all_gather(segment_ids[0], 'seq', axis=0, tiled=True)  21.7 us
    all_to_all x1, waiting for transfers between devices, body(): lax.all_to_all(out_part, 'seq', split_axis=0, concat_axis=1, tiled=True)  19.1 us
    all_to_all x1, waiting for transfers between devices, body(): lax.all_to_all(key_back, 'seq', split_axis=0, concat_axis=1, tiled=True)  12.3 us
    all_gather x1, waiting for transfers between devices, body(): lax.all_gather(stacked, ('seq', 'fsdp'), axis=0, tiled=True)  9.14 us
    unnamed x16, local copies, waits for them, and re-layouts  6.44 us
  transfers between devices with their start and end apart: 11, of which 9 were waited for; matrix products, arithmetic and copies ran while one was open for 13% of the time, Pallas kernels for 0%

commit v1 on v0

--- a/solution.py
+++ b/solution.py
@@ -181,7 +181,9 @@
     widen_by = heads_here // key_part.shape[1]
     key_part = jnp.repeat(key_part, widen_by, axis=1)
     value_part = jnp.repeat(value_part, widen_by, axis=1)
-    seg_all = lax.all_gather(segment_ids[0], "seq", axis=0, tiled=True)
+    seg_all = jnp.concatenate(
+        lax.all_to_all(jnp.stack([segment_ids[0]] * lax.axis_size("seq")), "seq", 0, 0), axis=0
+    )
     out_part, log_totals = attend(query_part, key_part, value_part, seg_all)
     context = lax.all_to_all(out_part, "seq", split_axis=0, concat_axis=1, tiled=True).reshape(
         1, rows_here, HEADS * HEAD_DIM

time: 249 us -> 253 us (1.016)
  blocking collectives: 21.7 us -> 0 us
  waiting for transfers between devices: 139 us -> 160 us
  starting transfers between devices: 31.6 us -> 35 us
    all_gather x1 -> x0, blocking collectives: 21.7 us -> none  [body(): seg_all = lax.all_gather(segment_ids[0], 'seq', axis=0, tiled=True)]
    all_gather x1, waiting for transfers between devices: 9.14 us -> 24.2 us  [body(): lax.all_gather(stacked, ('seq', 'fsdp'), axis=0, tiled=True)]
    all_to_all x0 -> x1, starting transfers between devices: none -> 6.32 us  [body(): lax.all_to_all(jnp.stack([segment_ids[0]] * lax.axis_size('seq')), 'seq',...]
    all_to_all x0 -> x1, waiting for transfers between devices: none -> 3.43 us  [body(): lax.all_to_all(jnp.stack([segment_ids[0]] * lax.axis_size('seq')), 'seq',...]
    all_to_all x1, starting transfers between devices: 6.32 us -> 3.47 us  [body(): lax.all_to_all(sent[0], 'seq', split_axis=1, concat_axis=0, tiled=True)]
    unnamed x16 -> x14, local copies, waits for them, and re-layouts: 6.44 us -> 6.43 us
  transfers between devices with their start and end apart: 11 -> 12, of which waited for: 9 -> 10; matrix products, arithmetic and copies ran while one was open for 13% -> 13% of each run, Pallas kernels for 0% -> 0%
where the time goes in v1:
time: 253 us; the launch traced here: 252 us
  waiting for transfers between devices  160 us (63%)
  starting transfers between devices  35 us (14%)
  matrix products  19.9 us (8%)
  local copies, waits for them, and re-layouts  18.7 us (7%)
  between operations  14 us (6%)
  other arithmetic  4.52 us (2%)
    reduce_scatter x1, waiting for transfers between devices, body(): lax.psum_scatter(lax.dot_general(columns, grad_kv, (((0,), (0,)), ((), ()...  34.4 us
    psum x1, waiting for transfers between devices, body(): grad_total = lax.psum(grad_shard, 'rep').astype(jnp.bfloat16)  27.7 us
    all_to_all x1, waiting for transfers between devices, body(): lax.all_to_all(sent[0], 'seq', split_axis=1, concat_axis=0, tiled=True)  27 us
    all_gather x1, waiting for transfers between devices, body(): lax.all_gather(stacked, ('seq', 'fsdp'), axis=0, tiled=True)  24.2 us
    all_to_all x1, waiting for transfers between devices, body(): lax.all_to_all(out_part, 'seq', split_axis=0, concat_axis=1, tiled=True)  19.1 us
    all_to_all x1, waiting for transfers between devices, body(): lax.all_to_all(key_back, 'seq', split_axis=0, concat_axis=1, tiled=True)  12.3 us
    unnamed x14, local copies, waits for them, and re-layouts  6.43 us
    all_to_all x1, starting transfers between devices, body(): lax.all_to_all(jnp.stack([segment_ids[0]] * lax.axis_size('seq')), 'seq',...  6.32 us
  transfers between devices with their start and end apart: 12, of which 10 were waited for; matrix products, arithmetic and copies ran while one was open for 13% of the time, Pallas kernels for 0%

profile of v1, /device:TPU:0, one launch (start us, length us, event | category | flops | bytes accessed | tf_op | source)
XLA Modules:
  0.0 252.1 jit_solution(1128379173121268920)
XLA Ops:
  7.2 0.0 copy-start
  7.2 0.0 all-gather.2.cloned.1.call-start
  7.2 1.9 pad_maximum_fusion
  9.2 0.0 all-gather.2.cloned.1.call-update
  9.2 1.2 stack.3
  10.4 6.3 %all-to-all-start = ((s32[4,1,128]{2,1,0:T(1,128)}), s32[4,1,128]{2,1,0:T(1,128)S(1)}, u32[]{:S(2)}, u32[]{:S(2)}) async-start(s32[4,1,128]{2,1,0:T(1,128)} %stack.3), calls=%async_computation | async-start | bytes 4096 | tf_op jit(solution)/shard_map/all_to_all | solution.py:185
  16.7 2.0 copy.45
  18.8 3.4 %all-to-all-done = s32[4,1,128]{2,1,0:T(1,128)S(1)} async-done(((s32[4,1,128]{2,1,0:T(1,128)}), s32[4,1,128]{2,1,0:T(1,128)S(1)}, u32[]{:S(2)}, u32[]{:S(2)}) %all-to-all-start) | async-done | bytes 2080 | tf_op jit(solution)/shard_map/all_to_all | solution.py:185
  22.2 3.5 %all-to-all-start.2 = ((bf16[128,16,128]{0,2,1:T(8,128)(2,1)}), bf16[128,16,128]{0,2,1:T(8,128)(2,1)S(1)}, u32[]{:S(2)}, u32[]{:S(2)}) async-start(bf16[128,16,128]{0,2,1:T(8,128)(2,1)} %bitcast.10), calls=%async_computation.2 | async-start | bytes 1048576 | tf_op jit(solution)/shard_map/all_to_all | solution.py:177
  25.7 2.0 copy.52
  27.7 27.0 %all-to-all-done.2 = bf16[128,16,128]{0,2,1:T(8,128)(2,1)S(1)} async-done(((bf16[128,16,128]{0,2,1:T(8,128)(2,1)}), bf16[128,16,128]{0,2,1:T(8,128)(2,1)S(1)}, u32[]{:S(2)}, u32[]{:S(2)}) %all-to-all-start.2) | async-done | bytes 524320 | tf_op jit(solution)/shard_map/all_to_all | solution.py:177
  54.7 3.5 %all-to-all-start.5 = ((bf16[128,16,128]{0,2,1:T(8,128)(2,1)}), bf16[128,16,128]{0,2,1:T(8,128)(2,1)S(1)}, u32[]{:S(2)}, u32[]{:S(2)}) async-start(bf16[128,16,128]{0,2,1:T(8,128)(2,1)} %bitcast.23), calls=%async_computation.5 | async-start | bytes 1048576 | tf_op jit(solution)/shard_map/all_to_all | solution.py:191
  58.2 24.2 %all-gather.2.cloned.1.call-done = bf16[2048,1024]{1,0:T(8,128)(2,1)} async-done(((bf16[256,1024]{1,0:T(8,128)(2,1)}), bf16[2048,1024]{1,0:T(8,128)(2,1)}) %all-gather.2.cloned.1.call-update) | async-done | bytes 4194320 | tf_op jit(solution)/shard_map/all_gather | solution.py:163
  82.4 0.0 copy-done
  82.4 3.5 %fusion.11 = bf16[128,1024]{0,1:T(8,128)(2,1)S(1)} fusion(bf16[2048,1024]{1,0:T(8,128)(2,1)} %all-gather.2.cloned.1.call-done, bf16[1,128,2048]{2,1,0:T(8,128)(2,1)S(1)} %copy-done), kind=kOutput, calls=%fused_computation.22 | convolution fusion | flops 537001984 | bytes 4980736 | tf_op jit(solution)/shard_map/dot_general | solution.py:161
  85.9 0.8 copy.44
  86.7 0.0 all-to-all-done.5
  86.7 3.3 %all-to-all-start.1 = ((bf16[128,4,128]{2,0,1:T(8,128)(2,1)}), bf16[128,4,128]{2,0,1:T(8,128)(2,1)S(1)}, u32[]{:S(2)}, u32[]{:S(2)}) async-start(bf16[128,4,128]{2,0,1:T(8,128)(2,1)} %copy.44), calls=%async_computation.1 | async-start | bytes 262144 | tf_op jit(solution)/shard_map/all_to_all | solution.py:178
  90.0 0.2 fusion.13
  90.3 0.3 copy.47
  90.5 0.3 copy.54
  90.8 0.8 copy.48
  91.6 4.8 %all-to-all-done.1 = bf16[128,4,128]{2,0,1:T(8,128)(2,1)S(1)} async-done(((bf16[128,4,128]{2,0,1:T(8,128)(2,1)}), bf16[128,4,128]{2,0,1:T(8,128)(2,1)S(1)}, u32[]{:S(2)}, u32[]{:S(2)}) %all-to-all-start.1) | async-done | bytes 131104 | tf_op jit(solution)/shard_map/all_to_all | solution.py:178
  96.4 3.3 %all-to-all-start.3 = ((bf16[128,4,128]{2,0,1:T(8,128)(2,1)}), bf16[128,4,128]{2,0,1:T(8,128)(2,1)S(1)}, u32[]{:S(2)}, u32[]{:S(2)}) async-start(bf16[128,4,128]{2,0,1:T(8,128)(2,1)} %copy.48), calls=%async_computation.3 | async-start | bytes 262144 | tf_op jit(solution)/shard_map/all_to_all | solution.py:179
  99.8 0.9 fusion.3
  100.7 1.0 select_reduce_fusion
  101.7 0.9 fusion.10
  102.7 1.2 copy.60
  103.9 1.8 all-to-all-done.3
  105.7 3.5 %all-to-all-start.8 = ((bf16[512,4,128]{2,1,0:T(4,128)(2,1)}), bf16[512,4,128]{2,1,0:T(4,128)(2,1)S(1)}, u32[]{:S(2)}, u32[]{:S(2)}) async-start(bf16[512,4,128]{2,1,0:T(4,128)(2,1)} %copy.60), calls=%async_computation.8 | async-start | bytes 1048576 | tf_op jit(solution)/shard_map/all_to_all | solution.py:204
  109.1 3.9 %fusion.12 = (f32[4,512]{1,0:T(4,128)S(1)}, bf16[4,512,128]{2,1,0:T(8,128)(2,1)S(1)}) fusion(bf16[4,128,4,128]{3,1,0,2:T(8,128)(2,1)S(1)} %copy.54, bf16[512,128]{1,0:T(8,128)(2,1)S(1)} %bitcast.112, f32[4,512,512]{2,1,0:T(8,128)} %copy-done.1, f32[4,512]{1,0:T(4,128)S(1)} %log_add_fusion, pred[512,512]{0,1:T(8,128)(4,1)S(1)} %fusion.13), kind=kOutput, calls=%fused_computation.24 | convolution fusion | flops 273938432 | bytes 5652480 | tf_op jit(solution)/shard_map/while/body/eval_jaxpr/while/body/hqk,khd->qhd/dot_general | solution.py:74
  113.0 1.4 fusion
  114.5 0.0 copy-start.3
  114.5 0.7 fusion.8
  115.2 0.6 copy-done.3
  115.8 1.2 copy.58
  117.0 5.2 %all-to-all-done.8 = bf16[512,4,128]{2,1,0:T(4,128)(2,1)S(1)} async-done(((bf16[512,4,128]{2,1,0:T(4,128)(2,1)}), bf16[512,4,128]{2,1,0:T(4,128)(2,1)S(1)}, u32[]{:S(2)}, u32[]{:S(2)}) %all-to-all-start.8) | async-done | bytes 524320 | tf_op jit(solution)/shard_map/all_to_all | solution.py:204
  122.3 3.5 %all-to-all-start.7 = ((bf16[512,4,128]{2,1,0:T(4,128)(2,1)}), bf16[512,4,128]{2,1,0:T(4,128)(2,1)S(1)}, u32[]{:S(2)}, u32[]{:S(2)}) async-start(bf16[512,4,128]{2,1,0:T(4,128)(2,1)} %copy.58), calls=%async_computation.7 | async-start | bytes 1048576 | tf_op jit(solution)/shard_map/all_to_all | solution.py:203
  125.7 0.2 reduce-scatter.2.cloned.1.call-start
  126.0 0.7 reduce_sum.48
  126.6 0.1 copy.61
  126.8 12.3 %all-to-all-done.7 = bf16[512,4,128]{2,1,0:T(4,128)(2,1)S(1)} async-done(((bf16[512,4,128]{2,1,0:T(4,128)(2,1)}), bf16[512,4,128]{2,1,0:T(4,128)(2,1)S(1)}, u32[]{:S(2)}, u32[]{:S(2)}) %all-to-all-start.7) | async-done | bytes 524320 | tf_op jit(solution)/shard_map/all_to_all | solution.py:203
  139.0 0.7 reduce_sum.45
  139.7 0.1 copy.59
  139.8 3.2 %convert_bitcast_fusion = bf16[2048,1024]{0,1:T(8,128)(2,1)} fusion(bf16[1,128,2048]{2,1,0:T(8,128)(2,1)S(1)} %copy-done, bf16[128,512]{0,1:T(8,128)(2,1)S(1)} %bitcast.99, bf16[128,512]{0,1:T(8,128)(2,1)S(1)} %bitcast.101), kind=kOutput, calls=%fused_computation.6 | convolution fusion | flops 539492352 | bytes 4980736 | tf_op jit(solution)/shard_map/dot_general | solution.py:228
  143.1 0.0 reduce-scatter.2.cloned.1.call-update
  143.1 1.2 copy.50
  144.3 3.5 %all-to-all-start.4 = ((bf16[512,4,128]{2,1,0:T(4,128)(2,1)}), bf16[512,4,128]{2,1,0:T(4,128)(2,1)S(1)}, u32[]{:S(2)}, u32[]{:S(2)}) async-start(bf16[512,4,128]{2,1,0:T(4,128)(2,1)} %copy.50), calls=%async_computation.4 | async-start | bytes 1048576 | tf_op jit(solution)/shard_map/all_to_all | solution.py:188
  147.8 0.9 fusion.9
  148.7 1.2 copy.56
  149.9 19.1 %all-to-all-done.4 = bf16[512,4,128]{2,1,0:T(4,128)(2,1)S(1)} async-done(((bf16[512,4,128]{2,1,0:T(4,128)(2,1)}), bf16[512,4,128]{2,1,0:T(4,128)(2,1)S(1)}, u32[]{:S(2)}, u32[]{:S(2)}) %all-to-all-start.4) | async-done | bytes 524320 | tf_op jit(solution)/shard_map/all_to_all | solution.py:188
  169.0 4.4 %all-to-all-start.6 = ((bf16[512,4,128]{2,1,0:T(4,128)(2,1)}), bf16[512,4,128]{2,1,0:T(4,128)(2,1)S(1)}, u32[]{:S(2)}, u32[]{:S(2)}) async-start(bf16[512,4,128]{2,1,0:T(4,128)(2,1)} %copy.56), calls=%async_computation.6 | async-start | bytes 1048576 | tf_op jit(solution)/shard_map/all_to_all | solution.py:202
  173.5 34.4 %reduce-scatter.2.cloned.1.call-done = bf16[256,1024]{0,1:T(8,128)(2,1)} async-done(((bf16[2048,1024]{0,1:T(8,128)(2,1)}), bf16[256,1024]{0,1:T(8,128)(2,1)}) %reduce-scatter.2.cloned.1.call-update) | async-done | bytes 524304 | tf_op jit(solution)/shard_map/reduce_scatter | solution.py:227
  207.9 0.0 all-reduce.2.cloned.1.call-update
  207.9 0.2 copy.51
  208.1 1.2 reshape.244
  209.3 0.0 all-to-all-done.6
  209.3 0.2 copy.57
  209.5 1.2 reshape.245
  210.7 4.5 %fusion.5 = bf16[1,128,2048]{2,1,0:T(8,128)(2,1)} fusion(bf16[2048,1024]{1,0:T(8,128)(2,1)} %all-gather.2.cloned.1.call-done, bf16[128,512]{0,1:T(8,128)(2,1)S(1)} %bitcast.100, bf16[128,512]{0,1:T(8,128)(2,1)S(1)} %bitcast.102), kind=kOutput, calls=%fused_computation.11 | convolution fusion | flops 537657344 | bytes 4980736 | tf_op jit(solution)/shard_map/dot_general | solution.py:219
  215.2 27.7 %all-reduce.2.cloned.1.call-done = bf16[256,1024]{0,1:T(8,128)(2,1)} async-done(((bf16[256,1024]{0,1:T(8,128)(2,1)}), bf16[256,1024]{0,1:T(8,128)(2,1)}) %all-reduce.2.cloned.1.call-update) | async-done | bytes 524304 | tf_op jit(solution)/shard_map/psum | solution.py:235
  242.8 1.1 fusion.25
  243.9 0.8 copy.63
  244.7 0.8 copy.62
  (10 shorter events, 0.1 us)
Async XLA Ops:
  7.2 75.2 %copy-start = (bf16[1,128,2048]{2,1,0:T(8,128)(2,1)S(1)}, bf16[1,128,2048]{2,1,0:T(8,128)(2,1)}, u32[]{:S(2)}) copy-start(bf16[1,128,2048]{2,1,0:T(8,128)(2,1)} %param.6) | copy-start | bytes 1572868
  7.2 75.2 %all-gather.2.cloned.1.call-start = ((), (), s32[]{:S(2)}) async-start(), calls=%async_computation.10 | async-start | bytes 4718592 | tf_op jit(solution)/shard_map/all_gather | solution.py:163
  10.4 11.8 %all-to-all-start = ((s32[4,1,128]{2,1,0:T(1,128)}), s32[4,1,128]{2,1,0:T(1,128)S(1)}, u32[]{:S(2)}, u32[]{:S(2)}) async-start(s32[4,1,128]{2,1,0:T(1,128)} %stack.3), calls=%async_computation | async-start | bytes 4096 | tf_op jit(solution)/shard_map/all_to_all | solution.py:185
  22.2 32.5 %all-to-all-start.2 = ((bf16[128,16,128]{0,2,1:T(8,128)(2,1)}), bf16[128,16,128]{0,2,1:T(8,128)(2,1)S(1)}, u32[]{:S(2)}, u32[]{:S(2)}) async-start(bf16[128,16,128]{0,2,1:T(8,128)(2,1)} %bitcast.10), calls=%async_computation.2 | async-start | bytes 1048576 | tf_op jit(solution)/shard_map/all_to_all | solution.py:177
  54.7 32.0 %all-to-all-start.5 = ((bf16[128,16,128]{0,2,1:T(8,128)(2,1)}), bf16[128,16,128]{0,2,1:T(8,128)(2,1)S(1)}, u32[]{:S(2)}, u32[]{:S(2)}) async-start(bf16[128,16,128]{0,2,1:T(8,128)(2,1)} %bitcast.23), calls=%async_computation.5 | async-start | bytes 1048576 | tf_op jit(solution)/shard_map/all_to_all | solution.py:191
  86.7 9.7 %all-to-all-start.1 = ((bf16[128,4,128]{2,0,1:T(8,128)(2,1)}), bf16[128,4,128]{2,0,1:T(8,128)(2,1)S(1)}, u32[]{:S(2)}, u32[]{:S(2)}) async-start(bf16[128,4,128]{2,0,1:T(8,128)(2,1)} %copy.44), calls=%async_computation.1 | async-start | bytes 262144 | tf_op jit(solution)/shard_map/all_to_all | solution.py:178
  96.4 9.2 %all-to-all-start.3 = ((bf16[128,4,128]{2,0,1:T(8,128)(2,1)}), bf16[128,4,128]{2,0,1:T(8,128)(2,1)S(1)}, u32[]{:S(2)}, u32[]{:S(2)}) async-start(bf16[128,4,128]{2,0,1:T(8,128)(2,1)} %copy.48), calls=%async_computation.3 | async-start | bytes 262144 | tf_op jit(solution)/shard_map/all_to_all | solution.py:179
  100.6 2.0 copy-start.1
  105.7 16.6 %all-to-all-start.8 = ((bf16[512,4,128]{2,1,0:T(4,128)(2,1)}), bf16[512,4,128]{2,1,0:T(4,128)(2,1)S(1)}, u32[]{:S(2)}, u32[]{:S(2)}) async-start(bf16[512,4,128]{2,1,0:T(4,128)(2,1)} %copy.60), calls=%async_computation.8 | async-start | bytes 1048576 | tf_op jit(solution)/shard_map/all_to_all | solution.py:204
  109.1 3.9 %copy-start.2 = (f32[4,512,512]{2,1,0:T(8,128)S(1)}, f32[4,512,512]{2,1,0:T(8,128)}, u32[]{:S(2)}) copy-start(f32[4,512,512]{2,1,0:T(8,128)} %copy-done.1) | copy-start | bytes 12582916
  114.5 1.4 copy-start.3
  122.3 16.8 %all-to-all-start.7 = ((bf16[512,4,128]{2,1,0:T(4,128)(2,1)}), bf16[512,4,128]{2,1,0:T(4,128)(2,1)S(1)}, u32[]{:S(2)}, u32[]{:S(2)}) async-start(bf16[512,4,128]{2,1,0:T(4,128)(2,1)} %copy.58), calls=%async_computation.7 | async-start | bytes 1048576 | tf_op jit(solution)/shard_map/all_to_all | solution.py:203
  125.7 82.2 %reduce-scatter.2.cloned.1.call-start = ((), (), s32[]{:S(2)}) async-start(), calls=%async_computation.11 | async-start | bytes 4718592 | tf_op jit(solution)/shard_map/reduce_scatter | solution.py:227
  143.1 4.7 %copy-start.4 = (bf16[4,512,512]{1,2,0:T(8,128)(2,1)S(1)}, bf16[4,512,512]{1,2,0:T(8,128)(2,1)}, u32[]{:S(2)}) copy-start(bf16[4,512,512]{1,2,0:T(8,128)(2,1)} %copy-done.3) | copy-start | bytes 6291460
  144.3 24.7 %all-to-all-start.4 = ((bf16[512,4,128]{2,1,0:T(4,128)(2,1)}), bf16[512,4,128]{2,1,0:T(4,128)(2,1)S(1)}, u32[]{:S(2)}, u32[]{:S(2)}) async-start(bf16[512,4,128]{2,1,0:T(4,128)(2,1)} %copy.50), calls=%async_computation.4 | async-start | bytes 1048576 | tf_op jit(solution)/shard_map/all_to_all | solution.py:188
  169.0 40.3 %all-to-all-start.6 = ((bf16[512,4,128]{2,1,0:T(4,128)(2,1)}), bf16[512,4,128]{2,1,0:T(4,128)(2,1)S(1)}, u32[]{:S(2)}, u32[]{:S(2)}) async-start(bf16[512,4,128]{2,1,0:T(4,128)(2,1)} %copy.56), calls=%async_computation.6 | async-start | bytes 1048576 | tf_op jit(solution)/shard_map/all_to_all | solution.py:202
  173.5 69.4 %all-reduce.2.cloned.1.call-start = ((), (), s32[]{:S(2)}) async-start(), calls=%async_computation.12 | async-start | bytes 1048576 | tf_op jit(solution)/shard_map/psum | solution.py:235
Sparse Core Ops, SparseCore 0:
  10.2 72.1 all-gather.1
  143.2 64.6 reduce-scatter.1
  210.2 32.5 all-reduce.1
